TPU v7x, 32 devices: a whole 2x2x4 slice. The times are simulated.
32 devices in a mesh: gx: 4 (over y, x), gy: 2 (over core), gz: 4 (over z).
Axes of the slice: x: 2, y: 2, z: 4, core: 2. Of those that a mesh axis runs over, the one named last changes fastest.
Arguments:
- field: bfloat16 [16, 64, 32, 512], P(None, 'gz', 'gy', 'gx'), may hold values from -6 to 6
- fine_taps: float32 [3, 9], replicated, may hold values from 0.1 to 0.6
- coarse_taps: float32 [3, 9], replicated, may hold values from 0.1 to 0.6
- top_kernel: bfloat16 [8, 4, 64, 2048], P('gz', 'gy', 'gx'), may hold values from -6 to 6
Outputs:
- applied: bfloat16 [16, 64, 32, 512], P(None, 'gz', 'gy', 'gx')
All inputs are finite; a program needn't handle non-finite values.
Results may differ from a plain program's by a relative error of at most 0.0047.
Values may be sent and summed in bfloat16 or wider, within the bound.
No kernel may reach another device: no remote copies, remote signals or barrier semaphores. Data moves between devices by JAX's collectives and lax.ppermute only.
A program may use at most 128 MiB of HBM per device.

v0:
```python
import jax
import jax.numpy as jnp
from jax import lax
from jax.sharding import PartitionSpec as P


def padded_2(cells, sides, width):
    for axis, dim in sides:
        count = lax.axis_size(axis)
        ends = count - 1
        head = lax.slice_in_dim(cells, 0, width, axis=dim)
        tail = lax.slice_in_dim(cells, cells.shape[dim] - width, cells.shape[dim], axis=dim)
        cells = jnp.concatenate(
            [
                lax.ppermute(tail, axis, [(i, (i + 1) % count) for i in range(ends)]),
                cells,
                lax.ppermute(head, axis, [((i + 1) % count, i) for i in range(ends)]),
            ],
            axis=dim,
        )
    return cells


def band_matrix(kernel_row, padded_length):
    length = padded_length - 8
    source = lax.broadcasted_iota(jnp.int32, (padded_length, length), 0)
    target = lax.broadcasted_iota(jnp.int32, (padded_length, length), 1)
    offset = source - target
    band = jnp.zeros((padded_length, length), jnp.float32)
    for tap in range(9):
        band = band + jnp.where(offset == tap, kernel_row[tap], 0.0)
    return band


def conv_padded(padded, kernel_row, along):
    length = padded.shape[along] - 8
    if along == padded.ndim - 1:
        band = band_matrix(kernel_row, padded.shape[along])
        return lax.dot_general(
            padded,
            band,
            (((along,), (0,)), ((), ())),
            precision=lax.Precision.HIGHEST,
            preferred_element_type=jnp.float32,
        )
    total = kernel_row[0] * lax.slice_in_dim(padded, 0, length, axis=along)
    for offset in range(1, 9):
        total = total + kernel_row[offset] * lax.slice_in_dim(
            padded, offset, offset + length, axis=along
        )
    return total


def separable_steps(values, kernel, rim_x, rim_y, rim_z):
    values = conv_padded(rim_x(values).astype(jnp.float32), kernel[2], 3)
    values = conv_padded(rim_y(values), kernel[1], 2)
    return conv_padded(rim_z(values), kernel[0], 1)


def restrict(values, factor):
    count, depth, rows, cols = values.shape
    shaped = values.reshape(
        count, depth // factor, factor, rows // factor, factor, cols // factor, factor
    )
    return shaped.mean(axis=(2, 4, 6))


def prolong(values, factor):
    values = jnp.repeat(values, factor, axis=1)
    values = jnp.repeat(values, factor, axis=2)
    return jnp.repeat(values, factor, axis=3)


def shards(field, fine_taps, coarse_taps, top_kernel):
    cells = field.astype(jnp.float32)
    coarse_cells = restrict(cells, 2)
    fine_part = separable_steps(
        field,
        fine_taps,
        lambda values: padded_2(values, (("gx", 3),), 4),
        lambda values: padded_2(values, (("gy", 2),), 4),
        lambda values: padded_2(values, (("gz", 1),), 4),
    )
    coarse_part = separable_steps(
        coarse_cells,
        coarse_taps,
        lambda values: padded_2(values.astype(jnp.bfloat16), (("gx", 3),), 4).astype(values.dtype),
        lambda values: padded_2(values.astype(jnp.bfloat16), (("gy", 2),), 4).astype(values.dtype),
        lambda values: padded_2(values.astype(jnp.bfloat16), (("gz", 1),), 4).astype(values.dtype),
    )
    top_in = restrict(coarse_cells, 4).astype(jnp.bfloat16)
    count, top_depth, top_rows, top_cols = top_in.shape
    along_x = lax.all_gather(top_in, "gx", axis=3, tiled=True)
    along_y = lax.all_gather(along_x, "gy", axis=2, tiled=True)
    along_z = lax.all_gather(along_y, "gz", axis=1, tiled=True)
    whole_top = along_z.reshape(count, -1)
    kernel_rows = top_kernel.reshape(-1, top_kernel.shape[3])
    top_part = lax.dot_general(
        whole_top, kernel_rows, (((1,), (1,)), ((), ())), preferred_element_type=jnp.float32
    )
    top_part = top_part.reshape(count, top_depth, top_rows, top_cols)
    coarse_total = coarse_part + prolong(top_part, 4)
    return (fine_part + prolong(coarse_total, 2)).astype(jnp.bfloat16)


def solution(mesh):
    return jax.shard_map(
        shards,
        mesh=mesh,
        in_specs=(P(None, "gz", "gy", "gx"), P(), P(), P("gz", "gy", "gx", None)),
        out_specs=P(None, "gz", "gy", "gx"),
        check_vma=False,
    )
```

profile of v0, /device:TPU:0, one launch (start us, length us, event | category | flops | bytes accessed | tf_op | source)
XLA Modules:
  0.0 185.4 jit_solution(7652606793168775549)
XLA Ops:
  0.0 9.9 %copy.23 = f32[16,16,16,128]{0,3,2,1:T(8,128)} copy(bf16[16,16,16,128]{3,2,1,0:T(8,128)(2,1)} %param.4) | data formatting | bytes 3145728 | tf_op jit(solution)/shard_map/reshape | solution.py:62
  9.9 11.7 %reduce_sum.18 = f32[16,8,8,64]{0,3,2,1:T(8,128)S(1)} reduce(f32[16,8,2,8,2,64,2]{0,6,5,4,3,2,1:T(2,128)} %bitcast.77, f32[]{:T(128)} %constant.13.clone.1), dimensions={2,4,6}, to_apply=%region_0.0 | reduce | flops 458752 | bytes 2359300 | tf_op jit(solution)/shard_map/reduce_sum | solution.py:65
  21.7 1.4 copy.24
  23.1 1.9 %fusion.209 = (bf16[16,8,8,64]{3,0,2,1:T(8,128)(2,1)S(1)}, f32[16,8,8,64]{3,0,2,1:T(8,128)}) fusion(f32[16,8,8,64]{3,0,2,1:T(8,128)} %copy.24), kind=kLoop, calls=%fused_computation.244 | loop fusion | flops 131072 | bytes 655360 | tf_op jit(solution)/shard_map/convert_element_type | solution.py:87
  25.0 0.7 copy-done.3
  25.7 0.9 fusion.215
  26.6 5.6 %collective-permute-start.6 = (bf16[16,8,8,4]{3,0,2,1:T(8,128)(2,1)}, bf16[16,8,8,4]{3,0,2,1:T(8,128)(2,1)}, u32[]{:S(2)}, u32[]{:S(2)}) collective-permute-start(bf16[16,8,8,4]{3,0,2,1:T(8,128)(2,1)} %get-tuple-element.17), channel_id=1, source_target_pairs={{0,8},{8,16},{16,24},{1,9},{9,17},{17,25},{2,10},{10,18},{18,26},{... | collective-permute-start | bytes 24584 | tf_op jit(solution)/shard_map/ppermute | solution.py:15
  32.1 1.3 collective-permute-start.7
  33.4 0.6 fusion.212
  34.0 2.5 %copy.37 = bf16[16,16,16,4]{2,1,3,0:T(8,128)(2,1)} copy(bf16[16,16,16,4]{3,2,1,0:T(8,128)(2,1)S(1)} %get-tuple-element.9) | data formatting | bytes 65536
  36.5 5.2 %collective-permute-start = (bf16[16,16,16,4]{2,1,3,0:T(8,128)(2,1)}, bf16[16,16,16,4]{2,1,3,0:T(8,128)(2,1)}, u32[]{:S(2)}, u32[]{:S(2)}) collective-permute-start(bf16[16,16,16,4]{2,1,3,0:T(8,128)(2,1)} %copy.37), channel_id=1, source_target_pairs={{0,8},{8,16},{16,24},{1,9},{9,17},{17,25},{2,10},{10,18},{18,26},{... | collective-permute-start | bytes 98312 | tf_op jit(solution)/shard_map/ppermute | solution.py:15
  41.7 2.5 %copy.38 = bf16[16,16,16,4]{2,1,3,0:T(8,128)(2,1)} copy(bf16[16,16,16,4]{3,2,1,0:T(8,128)(2,1)S(1)} %get-tuple-element.10) | data formatting | bytes 65536
  44.2 1.3 collective-permute-start.1
  45.5 0.7 fusion.218
  46.2 0.7 fusion.219
  46.9 0.7 fusion.216
  47.6 0.7 fusion.217
  48.3 1.7 copy.25
  49.9 0.5 reduce_sum.19
  50.5 9.9 %all_gather.9 = bf16[16,2,2,64]{0,2,1,3:T(2,128)(2,1)S(1)} all-gather(bf16[16,2,2,16]{0,2,1,3:T(2,128)(2,1)S(1)} %copy.26), channel_id=1, replica_groups=mesh['gx'=4,'gy'=2,'gz'=4] {'gx'}, dimensions={3}, use_global_device_ids=true | all-gather | bytes 10240 | tf_op jit(solution)/shard_map/all_gather | solution.py:93
  60.5 1.8 all_gather.10
  62.3 13.6 %all_gather.11 = bf16[16,8,4,64]{3,0,1,2:T(8,128)(2,1)S(1)} all-gather(bf16[16,2,4,64]{3,0,1,2:T(8,128)(2,1)S(1)} %all_gather.10), channel_id=1, replica_groups=mesh['gx'=4,'gy'=2,'gz'=4] {'gz'}, dimensions={1}, use_global_device_ids=true | all-gather | bytes 81920 | tf_op jit(solution)/shard_map/all_gather | solution.py:95
  76.2 7.2 %convolution_convert_fusion = bf16[16,8,8,64]{3,0,2,1:T(8,128)(2,1)S(1)} fusion(bf16[16,8,8,4]{3,0,2,1:T(8,128)(2,1)} %collective-permute-done.7, bf16[16,8,8,64]{3,0,2,1:T(8,128)(2,1)} %copy-done.3, bf16[16,8,8,4]{3,0,2,1:T(8,128)(2,1)} %collective-permute-done.6, f32[]{:T(128)} %bitcast.40, f32[]{:T(128)} %bitcast.39, f32[]{:T(128)} %bitcast.38, ...), kind=kOutput, calls=%fused_computation.80 | convolution fusion | flops 57255424 | bytes 278564 | tf_op jit(solution)/shard_map/dot_general | solution.py:39
  83.4 1.3 collective-permute-start.8
  84.7 1.3 collective-permute-start.9
  86.0 2.5 %copy.21 = bf16[16,16,16,4]{3,2,1,0:T(8,128)(2,1)S(1)} copy(bf16[16,16,16,4]{2,1,3,0:T(8,128)(2,1)} %collective-permute-done) | data formatting | bytes 65536 | tf_op jit(solution)/shard_map/ppermute | solution.py:15
  88.6 3.5 %copy.22 = bf16[16,16,16,4]{3,2,1,0:T(8,128)(2,1)} copy(bf16[16,16,16,4]{2,1,3,0:T(8,128)(2,1)} %collective-permute-done.1) | data formatting | bytes 65536 | tf_op jit(solution)/shard_map/ppermute | solution.py:17
  92.0 9.0 %fusion.46 = f32[16,16,16,128]{3,2,1,0:T(8,128)S(1)} fusion(bf16[16,16,16,4]{3,2,1,0:T(8,128)(2,1)} %copy.22, bf16[16,16,16,128]{3,2,1,0:T(8,128)(2,1)S(1)} %copy-done.2, bf16[16,16,16,4]{3,2,1,0:T(8,128)(2,1)S(1)} %copy.21, f32[]{:T(128)} %bitcast.10, f32[]{:T(128)} %bitcast.9, f32[]{:T(128)} %bitcast.8, f32[]{:T(128)} %bitcast.7, f32[]{:T(128)} %bitcast.6, ...), kind=kOutput, calls=%fused_computation.74 | convolution fusion | flops 859450368 | bytes 3211300 | tf_op jit(solution)/shard_map/dot_general | solution.py:39
  101.3 3.1 %collective-permute-start.2 = (f32[16,16,4,128]{3,2,1,0:T(4,128)S(1)}, f32[16,16,4,128]{3,2,1,0:T(4,128)S(1)}, u32[]{:S(2)}, u32[]{:S(2)}) collective-permute-start(f32[16,16,4,128]{3,2,1,0:T(4,128)S(1)} %get-tuple-element.7), channel_id=1, source_target_pairs={{0,4},{1,5},{2,6},{3,7},{8,12},{9,13},{10,14},{11,15},{16,20},{17,... | collective-permute-start | bytes 1572872 | tf_op jit(solution)/shard_map/ppermute | solution.py:15
  104.3 1.5 collective-permute-start.3
  106.0 5.7 %fusion.62 = bf16[16,8,8,64]{3,0,2,1:T(8,128)(2,1)S(1)} fusion(f32[16,8,16,64]{3,0,2,1:T(8,128)S(1)} %maximum_convert_fusion, f32[]{:T(128)} %bitcast.50, f32[]{:T(128)} %bitcast.49, f32[]{:T(128)} %bitcast.48, f32[]{:T(128)} %bitcast.47, f32[]{:T(128)} %bitcast.46, f32[]{:T(128)} %bitcast.45, f32[]{:T(128)} %bitcast.44, f32[]{:T(128)} %bitcast.43, f32[]{:T(128)} %bitcast.30), kind=kLoop, calls=%fused_computation.101 | loop fusion | flops 1179648 | bytes 2490404 | tf_op jit(solution)/shard_map/convert_element_type | solution.py:89
  111.7 0.7 fusion.213
  112.4 3.5 %collective-permute-start.10 = (bf16[16,4,8,64]{3,0,2,1:T(8,128)(2,1)}, bf16[16,4,8,64]{3,0,2,1:T(8,128)(2,1)S(1)}, u32[]{:S(2)}, u32[]{:S(2)}) collective-permute-start(bf16[16,4,8,64]{3,0,2,1:T(8,128)(2,1)} %get-tuple-element.13), channel_id=1, source_target_pairs={{0,1},{1,2},{2,3},{4,5},{5,6},{6,7},{8,9},{9,10},{10,11},{12,13},{... | collective-permute-start | bytes 196616 | tf_op jit(solution)/shard_map/ppermute | solution.py:15
  115.9 1.3 collective-permute-start.11
  117.3 8.9 %fusion.25 = f32[16,16,16,128]{3,2,1,0:T(8,128)S(1)} fusion(f32[16,16,16,128]{3,2,1,0:T(8,128)S(1)} %fusion.46, f32[16,16,4,128]{3,2,1,0:T(4,128)S(1)} %collective-permute-done.3, f32[16,16,4,128]{3,2,1,0:T(4,128)S(1)} %collective-permute-done.2, f32[]{:T(128)} %bitcast.20, f32[]{:T(128)} %bitcast.19, f32[]{:T(128)} %bitcast.18, f32[]{:T(128)} %bitcast.17, ...), kind=kLoop, calls=%fused_computation.49 | loop fusion | flops 13107200 | bytes 5242916 | tf_op jit(solution)/shard_map/add | solution.py:48
  126.2 1.0 fusion.210
  127.2 5.3 %collective-permute-start.4 = (f32[16,4,16,128]{3,2,1,0:T(8,128)}, f32[16,4,16,128]{3,2,1,0:T(8,128)}, u32[]{:S(2)}, u32[]{:S(2)}) collective-permute-start(f32[16,4,16,128]{3,2,1,0:T(8,128)} %get-tuple-element.5), channel_id=1, source_target_pairs={{0,1},{1,2},{2,3},{4,5},{5,6},{6,7},{8,9},{9,10},{10,11},{12,13},{... | collective-permute-start | bytes 1572872 | tf_op jit(solution)/shard_map/ppermute | solution.py:15
  132.6 1.3 collective-permute-start.5
  133.9 0.4 fusion.111
  134.5 1.5 broadcast_in_dim.120
  136.0 2.2 %copy.30 = f32[16,8,8,64]{3,0,2,1:T(8,128)S(1)} copy(f32[16,8,8,64]{0,2,3,1:T(8,128)} %bitcast.79) | data formatting | bytes 524288 | tf_op jit(solution)/shard_map/reshape | solution.py:71
  138.4 5.9 %fusion.53 = f32[16,8,8,64]{3,0,2,1:T(8,128)S(1)} fusion(f32[16,8,8,64]{3,0,2,1:T(8,128)S(1)} %copy.30, f32[16,16,8,64]{3,0,2,1:T(8,128)S(1)} %maximum_convert_fusion.1, f32[]{:T(128)} %bitcast.58, f32[]{:T(128)} %bitcast.57, f32[]{:T(128)} %bitcast.56, f32[]{:T(128)} %bitcast.55, f32[]{:T(128)} %bitcast.54, f32[]{:T(128)} %bitcast.53, f32[]{:T(128)} %bitcast.52, ...), kind=kLoop, calls=%fused_computation.83 | loop fusion | flops 1179648 | bytes 2883620 | tf_op jit(solution)/shard_map/add | solution.py:102
  144.5 0.4 broadcast_in_dim.121
  144.9 1.5 broadcast_in_dim.122
  146.4 6.7 %copy.32 = f32[16,16,16,64]{2,1,3,0:T(8,128)} copy(f32[16,16,16,64]{3,1,2,0:T(8,128)} %bitcast.80) | data formatting | bytes 2097152 | tf_op jit(solution)/shard_map/reshape | solution.py:70
  153.1 10.7 %broadcast_in_dim.123 = f32[16,16,16,64,2]{2,1,4,3,0:T(8,128)} broadcast(f32[16,16,16,64]{2,1,3,0:T(8,128)} %copy.32), dimensions={0,1,2,3} | broadcast | bytes 3145728 | tf_op jit(solution)/shard_map/broadcast_in_dim | solution.py:71
  163.8 11.4 %copy.33 = f32[16,16,16,128]{3,2,1,0:T(8,128)} copy(f32[16,16,16,128]{2,1,3,0:T(8,128)} %bitcast.76) | data formatting | bytes 4194304 | tf_op jit(solution)/shard_map/reshape | solution.py:71
  175.2 10.1 %fusion.5 = bf16[16,16,16,128]{3,2,1,0:T(8,128)(2,1)} fusion(f32[16,16,16,128]{3,2,1,0:T(8,128)} %copy.33, f32[16,16,16,128]{3,2,1,0:T(8,128)S(1)} %fusion.25, f32[16,4,16,128]{3,2,1,0:T(8,128)} %collective-permute-done.5, f32[16,4,16,128]{3,2,1,0:T(8,128)} %collective-permute-done.4, f32[]{:T(128)} %bitcast.28, f32[]{:T(128)} %bitcast.27, f32[]{:T(128)} %bitcast.26, ...), kind=kLoop, calls=%fused_computation.29 | loop fusion | flops 14155776 | bytes 6291492 | tf_op jit(solution)/shard_map/convert_element_type | solution.py:103
  (36 shorter events, 1.5 us)
Async XLA Ops:
  0.0 133.9 %copy-start = (bf16[2,2,16,2048]{3,2,1,0:T(8,128)(2,1)S(1)}, bf16[2,2,16,2048]{3,2,1,0:T(8,128)(2,1)}, u32[]{:S(2)}) copy-start(bf16[2,2,16,2048]{3,2,1,0:T(8,128)(2,1)} %param.7) | copy-start | bytes 786436
  21.7 11.8 %copy-start.2 = (bf16[16,16,16,128]{3,2,1,0:T(8,128)(2,1)S(1)}, bf16[16,16,16,128]{3,2,1,0:T(8,128)(2,1)}, u32[]{:S(2)}) copy-start(bf16[16,16,16,128]{3,2,1,0:T(8,128)(2,1)} %param.4) | copy-start | bytes 3145732
  25.0 0.7 copy-start.3
  26.6 49.6 %collective-permute-start.6 = (bf16[16,8,8,4]{3,0,2,1:T(8,128)(2,1)}, bf16[16,8,8,4]{3,0,2,1:T(8,128)(2,1)}, u32[]{:S(2)}, u32[]{:S(2)}) collective-permute-start(bf16[16,8,8,4]{3,0,2,1:T(8,128)(2,1)} %get-tuple-element.17), channel_id=1, source_target_pairs={{0,8},{8,16},{16,24},{1,9},{9,17},{17,25},{2,10},{10,18},{18,26},{... | collective-permute-start | bytes 24584 | tf_op jit(solution)/shard_map/ppermute | solution.py:15
  32.1 44.1 %collective-permute-start.7 = (bf16[16,8,8,4]{3,0,2,1:T(8,128)(2,1)}, bf16[16,8,8,4]{3,0,2,1:T(8,128)(2,1)}, u32[]{:S(2)}, u32[]{:S(2)}) collective-permute-start(bf16[16,8,8,4]{3,0,2,1:T(8,128)(2,1)} %get-tuple-element.18), channel_id=1, source_target_pairs={{8,0},{16,8},{24,16},{9,1},{17,9},{25,17},{10,2},{18,10},{26,18},{... | collective-permute-start | bytes 24584 | tf_op jit(solution)/shard_map/ppermute | solution.py:17
  34.0 11.5 %copy-start.4 = (f32[3,9]{1,0:T(4,128)S(1)}, f32[3,9]{1,0:T(4,128)}, u32[]{:S(2)}) copy-start(f32[3,9]{1,0:T(4,128)} %param.6) | copy-start | bytes 328
  34.0 12.9 %copy-start.5 = (f32[3,9]{1,0:T(4,128)S(1)}, f32[3,9]{1,0:T(4,128)}, u32[]{:S(2)}) copy-start(f32[3,9]{1,0:T(4,128)} %param.5) | copy-start | bytes 328
  36.5 49.5 %collective-permute-start = (bf16[16,16,16,4]{2,1,3,0:T(8,128)(2,1)}, bf16[16,16,16,4]{2,1,3,0:T(8,128)(2,1)}, u32[]{:S(2)}, u32[]{:S(2)}) collective-permute-start(bf16[16,16,16,4]{2,1,3,0:T(8,128)(2,1)} %copy.37), channel_id=1, source_target_pairs={{0,8},{8,16},{16,24},{1,9},{9,17},{17,25},{2,10},{10,18},{18,26},{... | collective-permute-start | bytes 98312 | tf_op jit(solution)/shard_map/ppermute | solution.py:15
  44.2 44.4 %collective-permute-start.1 = (bf16[16,16,16,4]{2,1,3,0:T(8,128)(2,1)}, bf16[16,16,16,4]{2,1,3,0:T(8,128)(2,1)}, u32[]{:S(2)}, u32[]{:S(2)}) collective-permute-start(bf16[16,16,16,4]{2,1,3,0:T(8,128)(2,1)} %copy.38), channel_id=1, source_target_pairs={{8,0},{16,8},{24,16},{9,1},{17,9},{25,17},{10,2},{18,10},{26,18},{... | collective-permute-start | bytes 98312 | tf_op jit(solution)/shard_map/ppermute | solution.py:17
  83.4 22.4 %collective-permute-start.8 = (bf16[16,8,4,64]{3,0,2,1:T(8,128)(2,1)S(1)}, bf16[16,8,4,64]{3,0,2,1:T(8,128)(2,1)S(1)}, u32[]{:S(2)}, u32[]{:S(2)}) collective-permute-start(bf16[16,8,4,64]{3,0,2,1:T(8,128)(2,1)S(1)} %get-tuple-element.15), channel_id=1, source_target_pairs={{0,4},{1,5},{2,6},{3,7},{8,12},{9,13},{10,14},{11,15},{16,20},{17,... | collective-permute-start | bytes 196616 | tf_op jit(solution)/shard_map/ppermute | solution.py:15
  84.7 21.1 %collective-permute-start.9 = (bf16[16,8,4,64]{3,0,2,1:T(8,128)(2,1)S(1)}, bf16[16,8,4,64]{3,0,2,1:T(8,128)(2,1)S(1)}, u32[]{:S(2)}, u32[]{:S(2)}) collective-permute-start(bf16[16,8,4,64]{3,0,2,1:T(8,128)(2,1)S(1)} %get-tuple-element.16), channel_id=1, source_target_pairs={{4,0},{5,1},{6,2},{7,3},{12,8},{13,9},{14,10},{15,11},{20,16},{21,... | collective-permute-start | bytes 196616 | tf_op jit(solution)/shard_map/ppermute | solution.py:17
  101.3 16.0 %collective-permute-start.2 = (f32[16,16,4,128]{3,2,1,0:T(4,128)S(1)}, f32[16,16,4,128]{3,2,1,0:T(4,128)S(1)}, u32[]{:S(2)}, u32[]{:S(2)}) collective-permute-start(f32[16,16,4,128]{3,2,1,0:T(4,128)S(1)} %get-tuple-element.7), channel_id=1, source_target_pairs={{0,4},{1,5},{2,6},{3,7},{8,12},{9,13},{10,14},{11,15},{16,20},{17,... | collective-permute-start | bytes 1572872 | tf_op jit(solution)/shard_map/ppermute | solution.py:15
  104.3 12.9 %collective-permute-start.3 = (f32[16,16,4,128]{3,2,1,0:T(4,128)S(1)}, f32[16,16,4,128]{3,2,1,0:T(4,128)S(1)}, u32[]{:S(2)}, u32[]{:S(2)}) collective-permute-start(f32[16,16,4,128]{3,2,1,0:T(4,128)S(1)} %get-tuple-element.8), channel_id=1, source_target_pairs={{4,0},{5,1},{6,2},{7,3},{12,8},{13,9},{14,10},{15,11},{20,16},{21,... | collective-permute-start | bytes 1572872 | tf_op jit(solution)/shard_map/ppermute | solution.py:17
  112.4 25.8 %collective-permute-start.10 = (bf16[16,4,8,64]{3,0,2,1:T(8,128)(2,1)}, bf16[16,4,8,64]{3,0,2,1:T(8,128)(2,1)S(1)}, u32[]{:S(2)}, u32[]{:S(2)}) collective-permute-start(bf16[16,4,8,64]{3,0,2,1:T(8,128)(2,1)} %get-tuple-element.13), channel_id=1, source_target_pairs={{0,1},{1,2},{2,3},{4,5},{5,6},{6,7},{8,9},{9,10},{10,11},{12,13},{... | collective-permute-start | bytes 196616 | tf_op jit(solution)/shard_map/ppermute | solution.py:15
  115.9 22.3 %collective-permute-start.11 = (bf16[16,4,8,64]{3,0,2,1:T(8,128)(2,1)S(1)}, bf16[16,4,8,64]{3,0,2,1:T(8,128)(2,1)S(1)}, u32[]{:S(2)}, u32[]{:S(2)}) collective-permute-start(bf16[16,4,8,64]{3,0,2,1:T(8,128)(2,1)S(1)} %get-tuple-element.14), channel_id=1, source_target_pairs={{1,0},{2,1},{3,2},{5,4},{6,5},{7,6},{9,8},{10,9},{11,10},{13,12},{... | collective-permute-start | bytes 196616 | tf_op jit(solution)/shard_map/ppermute | solution.py:17
  127.2 47.9 %collective-permute-start.4 = (f32[16,4,16,128]{3,2,1,0:T(8,128)}, f32[16,4,16,128]{3,2,1,0:T(8,128)}, u32[]{:S(2)}, u32[]{:S(2)}) collective-permute-start(f32[16,4,16,128]{3,2,1,0:T(8,128)} %get-tuple-element.5), channel_id=1, source_target_pairs={{0,1},{1,2},{2,3},{4,5},{5,6},{6,7},{8,9},{9,10},{10,11},{12,13},{... | collective-permute-start | bytes 1572872 | tf_op jit(solution)/shard_map/ppermute | solution.py:15
  132.6 42.6 %collective-permute-start.5 = (f32[16,4,16,128]{3,2,1,0:T(8,128)}, f32[16,4,16,128]{3,2,1,0:T(8,128)}, u32[]{:S(2)}, u32[]{:S(2)}) collective-permute-start(f32[16,4,16,128]{3,2,1,0:T(8,128)} %get-tuple-element.6), channel_id=1, source_target_pairs={{1,0},{2,1},{3,2},{5,4},{6,5},{7,6},{9,8},{10,9},{11,10},{13,12},{... | collective-permute-start | bytes 1572872 | tf_op jit(solution)/shard_map/ppermute | solution.py:17
  175.2 10.1 %copy-start.1 = (bf16[2,2,16,2048]{3,2,1,0:T(8,128)(2,1)S(1)}, bf16[2,2,16,2048]{3,2,1,0:T(8,128)(2,1)}, u32[]{:S(2)}) copy-start(bf16[2,2,16,2048]{3,2,1,0:T(8,128)(2,1)} %param.7) | copy-start | bytes 786436
where the time goes:
time: 187 us; the launch traced here: 185 us
  local copies, waits for them, and re-layouts  66 us (35%)
  other arithmetic  45.1 us (24%)
  starting transfers between devices  31.9 us (17%)
  blocking collectives  25.3 us (14%)
  matrix products  16.6 us (9%)
    ppermute x6, starting transfers between devices, padded_2(): lax.ppermute(tail, axis, [(i, (i + 1) % count) for i in range(ends)])  24 us
    dot_general x2, matrix products, conv_padded(): lax.dot_general(padded, band, (((along,), (0,)), ((), ())), precision=lax...  16.2 us
    all_gather x1, blocking collectives, shards(): along_z = lax.all_gather(along_y, 'gz', axis=1, tiled=True)  13.6 us
    reshape x2, local copies, waits for them, and re-layouts, prolong(): return jnp.repeat(values, factor, axis=3)  13.6 us
    reduce_sum x2, other arithmetic, restrict(): return shaped.mean(axis=(2, 4, 6))  12.3 us
    broadcast_in_dim x2, local copies, waits for them, and re-layouts, prolong(): return jnp.repeat(values, factor, axis=3)  12.1 us
    convert_element_type x1, other arithmetic, shards(): return (fine_part + prolong(coarse_total, 2)).astype(jnp.bfloat16)  10.1 us
    reshape x1, local copies, waits for them, and re-layouts, restrict(): values.reshape(count, depth // factor, factor, rows // factor, factor, co...  9.92 us
  transfers between devices with their start and end apart: 12, of which 0 were waited for; matrix products, arithmetic and copies ran while one was open for 49% of the time, Pallas kernels for 0%

commit v1 on v0

--- a/solution.py
+++ b/solution.py
@@ -92,7 +92,12 @@
     count, top_depth, top_rows, top_cols = top_in.shape
     along_x = lax.all_gather(top_in, "gx", axis=3, tiled=True)
     along_y = lax.all_gather(along_x, "gy", axis=2, tiled=True)
-    along_z = lax.all_gather(along_y, "gz", axis=1, tiled=True)
+    ring = [along_y]
+    for hop in range(3):
+        ring.append(lax.ppermute(ring[-1], "gz", [(dev, (dev + 1) % 4) for dev in range(4)]))
+    along_z = jnp.roll(
+        jnp.concatenate(ring[::-1], axis=1), (lax.axis_index("gz") + 1) * ring[0].shape[1], axis=1
+    )
     whole_top = along_z.reshape(count, -1)
     kernel_rows = top_kernel.reshape(-1, top_kernel.shape[3])
     top_part = lax.dot_general(

time: 187 us -> 181 us (0.968)
  blocking collectives: 25.3 us -> 13.2 us
  starting transfers between devices: 31.9 us -> 34.8 us
    all_gather x1 -> x0, blocking collectives: 13.6 us -> none  [shards(): along_z = lax.all_gather(along_y, 'gz', axis=1, tiled=True)]
    ppermute x0 -> x3, starting transfers between devices: none -> 4.87 us  [shards(): lax.ppermute(ring[-1], 'gz', [(dev, (dev + 1) % 4) for dev in range(4)])]
    ppermute x6, starting transfers between devices: 24 us -> 22 us  [padded_2(): lax.ppermute(tail, axis, [(i, (i + 1) % count) for i in range(ends)])]
    slice x6, local copies, waits for them, and re-layouts: 3.37 us -> 5.26 us  [padded_2(): lax.slice_in_dim(cells, cells.shape[dim] - width, cells.shape[dim], axis=...]
    unnamed x14 -> x29, local copies, waits for them, and re-layouts: 5.63 us -> 5.62 us
  transfers between devices with their start and end apart: 12 -> 15, of which waited for: 0 -> 1; matrix products, arithmetic and copies ran while one was open for 49% -> 53% of each run, Pallas kernels for 0% -> 0%
where the time goes in v1:
time: 181 us; the launch traced here: 178 us
  local copies, waits for them, and re-layouts  66.3 us (37%)
  other arithmetic  46.2 us (26%)
  starting transfers between devices  34.8 us (19%)
  matrix products  16.7 us (9%)
  blocking collectives  13.2 us (7%)
    ppermute x6, starting transfers between devices, padded_2(): lax.ppermute(tail, axis, [(i, (i + 1) % count) for i in range(ends)])  22 us
    dot_general x2, matrix products, conv_padded(): lax.dot_general(padded, band, (((along,), (0,)), ((), ())), precision=lax...  16.3 us
    reshape x2, local copies, waits for them, and re-layouts, prolong(): return jnp.repeat(values, factor, axis=3)  13.6 us
    reduce_sum x2, other arithmetic, restrict(): return shaped.mean(axis=(2, 4, 6))  12.3 us
    broadcast_in_dim x2, local copies, waits for them, and re-layouts, prolong(): return jnp.repeat(values, factor, axis=3)  12.2 us
    all_gather x1, blocking collectives, shards(): along_x = lax.all_gather(top_in, 'gx', axis=3, tiled=True)  11.4 us
    add x1, other arithmetic, conv_padded(): total + kernel_row[offset] * lax.slice_in_dim(padded, offset, offset + le...  10.5 us
    convert_element_type x1, other arithmetic, shards(): return (fine_part + prolong(coarse_total, 2)).astype(jnp.bfloat16)  10.3 us
  transfers between devices with their start and end apart: 15, of which 1 were waited for; matrix products, arithmetic and copies ran while one was open for 53% of the time, Pallas kernels for 0%

profile of v1, /device:TPU:0, one launch (start us, length us, event | category | flops | bytes accessed | tf_op | source)
XLA Modules:
  0.0 177.9 jit_solution(6073491595189725051)
XLA Ops:
  0.0 9.9 %copy.23 = f32[16,16,16,128]{0,3,2,1:T(8,128)} copy(bf16[16,16,16,128]{3,2,1,0:T(8,128)(2,1)} %param.4) | data formatting | bytes 3145728 | tf_op jit(solution)/shard_map/reshape | solution.py:62
  9.9 11.7 %reduce_sum.18 = f32[16,8,8,64]{0,3,2,1:T(8,128)S(1)} reduce(f32[16,8,2,8,2,64,2]{0,6,5,4,3,2,1:T(2,128)} %bitcast.77, f32[]{:T(128)} %constant.17.clone.1), dimensions={2,4,6}, to_apply=%region_0.0 | reduce | flops 458752 | bytes 2359300 | tf_op jit(solution)/shard_map/reduce_sum | solution.py:65
  21.7 0.6 copy.24
  22.3 0.9 fusion.209
  23.2 0.9 fusion.215
  24.1 5.6 %collective-permute-start.6 = (bf16[16,8,8,4]{3,0,2,1:T(8,128)(2,1)}, bf16[16,8,8,4]{3,0,2,1:T(8,128)(2,1)}, u32[]{:S(2)}, u32[]{:S(2)}) collective-permute-start(bf16[16,8,8,4]{3,0,2,1:T(8,128)(2,1)} %get-tuple-element.17), channel_id=1, source_target_pairs={{0,8},{8,16},{16,24},{1,9},{9,17},{17,25},{2,10},{10,18},{18,26},{... | collective-permute-start | bytes 24584 | tf_op jit(solution)/shard_map/ppermute | solution.py:15
  29.7 1.3 collective-permute-start.7
  31.0 1.7 copy.25
  33.3 11.4 %all_gather.6 = bf16[16,2,2,64]{0,2,1,3:T(2,128)(2,1)S(1)} all-gather(bf16[16,2,2,16]{0,2,1,3:T(2,128)(2,1)S(1)} %copy.26), channel_id=1, replica_groups=mesh['gx'=4,'gy'=2,'gz'=4] {'gx'}, dimensions={3}, use_global_device_ids=true | all-gather | bytes 10240 | tf_op jit(solution)/shard_map/all_gather | solution.py:93
  44.8 1.8 %all_gather.7 = bf16[16,2,4,64]{3,0,1,2:T(8,128)(2,1)S(1)} all-gather(bf16[16,2,2,64]{3,0,1,2:T(8,128)(2,1)S(1)} %copy.27), channel_id=1, replica_groups=mesh['gx'=4,'gy'=2,'gz'=4] {'gy'}, dimensions={2}, use_global_device_ids=true | all-gather | bytes 24576 | tf_op jit(solution)/shard_map/all_gather | solution.py:94
  46.6 1.6 collective-permute-start.12
  48.2 1.6 fusion.212
  49.8 3.0 %copy.37 = bf16[16,16,16,4]{2,1,3,0:T(8,128)(2,1)S(1)} copy(bf16[16,16,16,4]{3,2,1,0:T(8,128)(2,1)} %get-tuple-element.9) | data formatting | bytes 65536
  52.8 3.7 %collective-permute-start = (bf16[16,16,16,4]{2,1,3,0:T(8,128)(2,1)S(1)}, bf16[16,16,16,4]{2,1,3,0:T(8,128)(2,1)S(1)}, u32[]{:S(2)}, u32[]{:S(2)}) collective-permute-start(bf16[16,16,16,4]{2,1,3,0:T(8,128)(2,1)S(1)} %copy.37), channel_id=1, source_target_pairs={{0,8},{8,16},{16,24},{1,9},{9,17},{17,25},{2,10},{10,18},{18,26},{... | collective-permute-start | bytes 98312 | tf_op jit(solution)/shard_map/ppermute | solution.py:15
  56.5 1.7 copy.38
  58.2 1.3 collective-permute-start.1
  59.6 0.7 fusion.218
  60.3 0.7 fusion.219
  61.0 0.7 fusion.216
  61.7 0.7 fusion.217
  62.4 7.0 %convolution_convert_fusion = bf16[16,8,8,64]{3,0,2,1:T(8,128)(2,1)S(1)} fusion(bf16[16,8,8,4]{3,0,2,1:T(8,128)(2,1)} %collective-permute-done.7, bf16[16,8,8,64]{3,0,2,1:T(8,128)(2,1)S(1)} %copy-done.6, bf16[16,8,8,4]{3,0,2,1:T(8,128)(2,1)} %collective-permute-done.6, f32[]{:T(128)} %bitcast.40, f32[]{:T(128)} %bitcast.39, f32[]{:T(128)} %bitcast.38, ...), kind=kOutput, calls=%fused_computation.80 | convolution fusion | flops 57255424 | bytes 278564 | tf_op jit(solution)/shard_map/dot_general | solution.py:39
  69.3 0.7 fusion.214
  70.1 1.5 collective-permute-start.8
  71.5 1.3 collective-permute-start.9
  72.8 1.6 collective-permute-start.13
  74.5 1.6 copy.21
  76.1 3.5 %copy.22 = bf16[16,16,16,4]{3,2,1,0:T(8,128)(2,1)} copy(bf16[16,16,16,4]{2,1,3,0:T(8,128)(2,1)} %collective-permute-done.1) | data formatting | bytes 65536 | tf_op jit(solution)/shard_map/ppermute | solution.py:17
  79.6 9.3 %fusion.46 = f32[16,16,16,128]{3,2,1,0:T(8,128)S(1)} fusion(bf16[16,16,16,4]{3,2,1,0:T(8,128)(2,1)} %copy.22, bf16[16,16,16,128]{3,2,1,0:T(8,128)(2,1)S(1)} %copy-done.2, bf16[16,16,16,4]{3,2,1,0:T(8,128)(2,1)S(1)} %copy.21, f32[]{:T(128)} %bitcast.10, f32[]{:T(128)} %bitcast.9, f32[]{:T(128)} %bitcast.8, f32[]{:T(128)} %bitcast.7, f32[]{:T(128)} %bitcast.6, ...), kind=kOutput, calls=%fused_computation.74 | convolution fusion | flops 859450368 | bytes 3211300 | tf_op jit(solution)/shard_map/dot_general | solution.py:39
  88.9 1.6 collective-permute-start.14
  90.8 2.5 %collective-permute-start.2 = (f32[16,16,4,128]{3,2,1,0:T(4,128)S(1)}, f32[16,16,4,128]{3,2,1,0:T(4,128)S(1)}, u32[]{:S(2)}, u32[]{:S(2)}) collective-permute-start(f32[16,16,4,128]{3,2,1,0:T(4,128)S(1)} %get-tuple-element.7), channel_id=1, source_target_pairs={{0,4},{1,5},{2,6},{3,7},{8,12},{9,13},{10,14},{11,15},{16,20},{17,... | collective-permute-start | bytes 1572872 | tf_op jit(solution)/shard_map/ppermute | solution.py:15
  93.3 1.5 collective-permute-start.3
  95.5 6.1 %fusion.62 = bf16[16,8,8,64]{3,0,2,1:T(8,128)(2,1)S(1)} fusion(f32[16,8,16,64]{3,0,2,1:T(8,128)S(1)} %maximum_convert_fusion, f32[]{:T(128)} %bitcast.50, f32[]{:T(128)} %bitcast.49, f32[]{:T(128)} %bitcast.48, f32[]{:T(128)} %bitcast.47, f32[]{:T(128)} %bitcast.46, f32[]{:T(128)} %bitcast.45, f32[]{:T(128)} %bitcast.44, f32[]{:T(128)} %bitcast.43, f32[]{:T(128)} %bitcast.30), kind=kLoop, calls=%fused_computation.101 | loop fusion | flops 1179648 | bytes 2490404 | tf_op jit(solution)/shard_map/convert_element_type | solution.py:89
  101.6 0.7 fusion.213
  102.3 3.4 %collective-permute-start.10 = (bf16[16,4,8,64]{3,0,2,1:T(8,128)(2,1)}, bf16[16,4,8,64]{3,0,2,1:T(8,128)(2,1)S(1)}, u32[]{:S(2)}, u32[]{:S(2)}) collective-permute-start(bf16[16,4,8,64]{3,0,2,1:T(8,128)(2,1)} %get-tuple-element.13), channel_id=1, source_target_pairs={{0,1},{1,2},{2,3},{4,5},{5,6},{6,7},{8,9},{9,10},{10,11},{12,13},{... | collective-permute-start | bytes 196616 | tf_op jit(solution)/shard_map/ppermute | solution.py:15
  105.7 1.3 collective-permute-start.11
  107.1 0.8 copy-done.7
  107.9 10.5 %fusion.25 = f32[16,16,16,128]{3,2,1,0:T(8,128)S(1)} fusion(f32[16,16,16,128]{3,2,1,0:T(8,128)S(1)} %copy-done.4, f32[16,16,4,128]{3,2,1,0:T(4,128)} %copy-done.7, f32[16,16,4,128]{3,2,1,0:T(4,128)S(1)} %collective-permute-done.2, f32[]{:T(128)} %bitcast.20, f32[]{:T(128)} %bitcast.19, f32[]{:T(128)} %bitcast.18, f32[]{:T(128)} %bitcast.17, f32[]{:T(128)} %bitcast.16, ...), kind=kLoop, calls=%fused_computation.49 | loop fusion | flops 13107200 | bytes 5242916 | tf_op jit(solution)/shard_map/add | solution.py:48
  118.4 1.0 fusion.210
  119.5 5.3 %collective-permute-start.4 = (f32[16,4,16,128]{3,2,1,0:T(8,128)}, f32[16,4,16,128]{3,2,1,0:T(8,128)}, u32[]{:S(2)}, u32[]{:S(2)}) collective-permute-start(f32[16,4,16,128]{3,2,1,0:T(8,128)} %get-tuple-element.5), channel_id=1, source_target_pairs={{0,1},{1,2},{2,3},{4,5},{5,6},{6,7},{8,9},{9,10},{10,11},{12,13},{... | collective-permute-start | bytes 1572872 | tf_op jit(solution)/shard_map/ppermute | solution.py:15
  124.8 1.3 collective-permute-start.5
  126.7 1.5 broadcast_in_dim.120
  128.2 2.2 %copy.30 = f32[16,8,8,64]{3,0,2,1:T(8,128)S(1)} copy(f32[16,8,8,64]{0,2,3,1:T(8,128)} %bitcast.79) | data formatting | bytes 524288 | tf_op jit(solution)/shard_map/reshape | solution.py:71
  130.6 5.8 %fusion.53 = f32[16,8,8,64]{3,0,2,1:T(8,128)S(1)} fusion(f32[16,8,8,64]{3,0,2,1:T(8,128)S(1)} %copy.30, f32[16,16,8,64]{3,0,2,1:T(8,128)S(1)} %maximum_convert_fusion.1, f32[]{:T(128)} %bitcast.58, f32[]{:T(128)} %bitcast.57, f32[]{:T(128)} %bitcast.56, f32[]{:T(128)} %bitcast.55, f32[]{:T(128)} %bitcast.54, f32[]{:T(128)} %bitcast.53, f32[]{:T(128)} %bitcast.52, ...), kind=kLoop, calls=%fused_computation.83 | loop fusion | flops 1179648 | bytes 2883620 | tf_op jit(solution)/shard_map/add | solution.py:107
  137.1 1.5 broadcast_in_dim.122
  138.6 6.7 %copy.32 = f32[16,16,16,64]{2,1,3,0:T(8,128)} copy(f32[16,16,16,64]{3,1,2,0:T(8,128)} %bitcast.80) | data formatting | bytes 2097152 | tf_op jit(solution)/shard_map/reshape | solution.py:70
  145.3 10.7 %broadcast_in_dim.123 = f32[16,16,16,64,2]{2,1,4,3,0:T(8,128)} broadcast(f32[16,16,16,64]{2,1,3,0:T(8,128)} %copy.32), dimensions={0,1,2,3} | broadcast | bytes 3145728 | tf_op jit(solution)/shard_map/broadcast_in_dim | solution.py:71
  156.0 11.4 %copy.33 = f32[16,16,16,128]{3,2,1,0:T(8,128)} copy(f32[16,16,16,128]{2,1,3,0:T(8,128)} %bitcast.76) | data formatting | bytes 4194304 | tf_op jit(solution)/shard_map/reshape | solution.py:71
  167.4 10.3 %fusion.5 = bf16[16,16,16,128]{3,2,1,0:T(8,128)(2,1)} fusion(f32[16,16,16,128]{3,2,1,0:T(8,128)} %copy.33, f32[16,16,16,128]{3,2,1,0:T(8,128)S(1)} %fusion.25, f32[16,4,16,128]{3,2,1,0:T(8,128)} %collective-permute-done.5, f32[16,4,16,128]{3,2,1,0:T(8,128)} %collective-permute-done.4, f32[]{:T(128)} %bitcast.28, f32[]{:T(128)} %bitcast.27, f32[]{:T(128)} %bitcast.26, ...), kind=kLoop, calls=%fused_computation.29 | loop fusion | flops 14155776 | bytes 6291492 | tf_op jit(solution)/shard_map/convert_element_type | solution.py:108
  (58 shorter events, 3.1 us)
Async XLA Ops:
  0.0 126.1 %copy-start = (bf16[2,2,16,2048]{3,2,1,0:T(8,128)(2,1)S(1)}, bf16[2,2,16,2048]{3,2,1,0:T(8,128)(2,1)}, u32[]{:S(2)}) copy-start(bf16[2,2,16,2048]{3,2,1,0:T(8,128)(2,1)} %param.7) | copy-start | bytes 786436
  23.2 7.8 %copy-start.5 = (bf16[16,8,8,64]{3,0,2,1:T(8,128)(2,1)}, bf16[16,8,8,64]{3,0,2,1:T(8,128)(2,1)S(1)}, u32[]{:S(2)}) copy-start(bf16[16,8,8,64]{3,0,2,1:T(8,128)(2,1)S(1)} %get-tuple-element.11) | copy-start | bytes 393220
  24.1 38.3 %collective-permute-start.6 = (bf16[16,8,8,4]{3,0,2,1:T(8,128)(2,1)}, bf16[16,8,8,4]{3,0,2,1:T(8,128)(2,1)}, u32[]{:S(2)}, u32[]{:S(2)}) collective-permute-start(bf16[16,8,8,4]{3,0,2,1:T(8,128)(2,1)} %get-tuple-element.17), channel_id=1, source_target_pairs={{0,8},{8,16},{16,24},{1,9},{9,17},{17,25},{2,10},{10,18},{18,26},{... | collective-permute-start | bytes 24584 | tf_op jit(solution)/shard_map/ppermute | solution.py:15
  29.7 32.7 %collective-permute-start.7 = (bf16[16,8,8,4]{3,0,2,1:T(8,128)(2,1)}, bf16[16,8,8,4]{3,0,2,1:T(8,128)(2,1)}, u32[]{:S(2)}, u32[]{:S(2)}) collective-permute-start(bf16[16,8,8,4]{3,0,2,1:T(8,128)(2,1)} %get-tuple-element.18), channel_id=1, source_target_pairs={{8,0},{16,8},{24,16},{9,1},{17,9},{25,17},{10,2},{18,10},{26,18},{... | collective-permute-start | bytes 24584 | tf_op jit(solution)/shard_map/ppermute | solution.py:17
  31.0 17.2 %copy-start.2 = (bf16[16,16,16,128]{3,2,1,0:T(8,128)(2,1)S(1)}, bf16[16,16,16,128]{3,2,1,0:T(8,128)(2,1)}, u32[]{:S(2)}) copy-start(bf16[16,16,16,128]{3,2,1,0:T(8,128)(2,1)} %param.4) | copy-start | bytes 3145732
  46.6 26.2 %collective-permute-start.12 = (bf16[16,2,4,64]{3,0,1,2:T(8,128)(2,1)S(1)}, bf16[16,2,4,64]{3,0,1,2:T(8,128)(2,1)S(1)}, u32[]{:S(2)}, u32[]{:S(2)}) collective-permute-start(bf16[16,2,4,64]{3,0,1,2:T(8,128)(2,1)S(1)} %all_gather.7), channel_id=1, source_target_pairs={{0,1},{1,2},{2,3},{3,0},{4,5},{5,6},{6,7},{7,4},{8,9},{9,10},{10,1... | collective-permute-start | bytes 49160 | tf_op jit(solution)/shard_map/ppermute | solution.py:97
  49.8 9.8 %copy-start.8 = (f32[3,9]{1,0:T(4,128)S(1)}, f32[3,9]{1,0:T(4,128)}, u32[]{:S(2)}) copy-start(f32[3,9]{1,0:T(4,128)} %param.6) | copy-start | bytes 328
  49.8 11.2 %copy-start.9 = (f32[3,9]{1,0:T(4,128)S(1)}, f32[3,9]{1,0:T(4,128)}, u32[]{:S(2)}) copy-start(f32[3,9]{1,0:T(4,128)} %param.5) | copy-start | bytes 328
  49.8 12.6 %copy-start.6 = (bf16[16,8,8,64]{3,0,2,1:T(8,128)(2,1)S(1)}, bf16[16,8,8,64]{3,0,2,1:T(8,128)(2,1)}, u32[]{:S(2)}) copy-start(bf16[16,8,8,64]{3,0,2,1:T(8,128)(2,1)} %copy-done.5) | copy-start | bytes 393220
  52.8 21.7 %collective-permute-start = (bf16[16,16,16,4]{2,1,3,0:T(8,128)(2,1)S(1)}, bf16[16,16,16,4]{2,1,3,0:T(8,128)(2,1)S(1)}, u32[]{:S(2)}, u32[]{:S(2)}) collective-permute-start(bf16[16,16,16,4]{2,1,3,0:T(8,128)(2,1)S(1)} %copy.37), channel_id=1, source_target_pairs={{0,8},{8,16},{16,24},{1,9},{9,17},{17,25},{2,10},{10,18},{18,26},{... | collective-permute-start | bytes 98312 | tf_op jit(solution)/shard_map/ppermute | solution.py:15
  58.2 17.8 %collective-permute-start.1 = (bf16[16,16,16,4]{2,1,3,0:T(8,128)(2,1)S(1)}, bf16[16,16,16,4]{2,1,3,0:T(8,128)(2,1)}, u32[]{:S(2)}, u32[]{:S(2)}) collective-permute-start(bf16[16,16,16,4]{2,1,3,0:T(8,128)(2,1)S(1)} %copy.38), channel_id=1, source_target_pairs={{8,0},{16,8},{24,16},{9,1},{17,9},{25,17},{10,2},{18,10},{26,18},{... | collective-permute-start | bytes 98312 | tf_op jit(solution)/shard_map/ppermute | solution.py:17
  70.1 25.2 %collective-permute-start.8 = (bf16[16,8,4,64]{3,0,2,1:T(8,128)(2,1)}, bf16[16,8,4,64]{3,0,2,1:T(8,128)(2,1)S(1)}, u32[]{:S(2)}, u32[]{:S(2)}) collective-permute-start(bf16[16,8,4,64]{3,0,2,1:T(8,128)(2,1)} %get-tuple-element.15), channel_id=1, source_target_pairs={{0,4},{1,5},{2,6},{3,7},{8,12},{9,13},{10,14},{11,15},{16,20},{17,... | collective-permute-start | bytes 196616 | tf_op jit(solution)/shard_map/ppermute | solution.py:15
  71.5 23.8 %collective-permute-start.9 = (bf16[16,8,4,64]{3,0,2,1:T(8,128)(2,1)}, bf16[16,8,4,64]{3,0,2,1:T(8,128)(2,1)S(1)}, u32[]{:S(2)}, u32[]{:S(2)}) collective-permute-start(bf16[16,8,4,64]{3,0,2,1:T(8,128)(2,1)} %get-tuple-element.16), channel_id=1, source_target_pairs={{4,0},{5,1},{6,2},{7,3},{12,8},{13,9},{14,10},{15,11},{20,16},{21,... | collective-permute-start | bytes 196616 | tf_op jit(solution)/shard_map/ppermute | solution.py:17
  72.8 16.0 %collective-permute-start.13 = (bf16[16,2,4,64]{3,0,1,2:T(8,128)(2,1)S(1)}, bf16[16,2,4,64]{3,0,1,2:T(8,128)(2,1)S(1)}, u32[]{:S(2)}, u32[]{:S(2)}) collective-permute-start(bf16[16,2,4,64]{3,0,1,2:T(8,128)(2,1)S(1)} %collective-permute-done.12), channel_id=1, source_target_pairs={{0,1},{1,2},{2,3},{3,0},{4,5},{5,6},{6,7},{7,4},{8,9},{9,10},{10,1... | collective-permute-start | bytes 49160 | tf_op jit(solution)/shard_map/ppermute | solution.py:97
  88.9 1.6 copy-start.3
  88.9 6.0 %collective-permute-start.14 = (bf16[16,2,4,64]{3,0,1,2:T(8,128)(2,1)S(1)}, bf16[16,2,4,64]{3,0,1,2:T(8,128)(2,1)S(1)}, u32[]{:S(2)}, u32[]{:S(2)}) collective-permute-start(bf16[16,2,4,64]{3,0,1,2:T(8,128)(2,1)S(1)} %collective-permute-done.13), channel_id=1, source_target_pairs={{0,1},{1,2},{2,3},{3,0},{4,5},{5,6},{6,7},{7,4},{8,9},{9,10},{10,1... | collective-permute-start | bytes 49160 | tf_op jit(solution)/shard_map/ppermute | solution.py:97
  90.8 16.3 %collective-permute-start.2 = (f32[16,16,4,128]{3,2,1,0:T(4,128)S(1)}, f32[16,16,4,128]{3,2,1,0:T(4,128)S(1)}, u32[]{:S(2)}, u32[]{:S(2)}) collective-permute-start(f32[16,16,4,128]{3,2,1,0:T(4,128)S(1)} %get-tuple-element.7), channel_id=1, source_target_pairs={{0,4},{1,5},{2,6},{3,7},{8,12},{9,13},{10,14},{11,15},{16,20},{17,... | collective-permute-start | bytes 1572872 | tf_op jit(solution)/shard_map/ppermute | solution.py:15
  93.3 13.7 %collective-permute-start.3 = (f32[16,16,4,128]{3,2,1,0:T(4,128)S(1)}, f32[16,16,4,128]{3,2,1,0:T(4,128)S(1)}, u32[]{:S(2)}, u32[]{:S(2)}) collective-permute-start(f32[16,16,4,128]{3,2,1,0:T(4,128)S(1)} %get-tuple-element.8), channel_id=1, source_target_pairs={{4,0},{5,1},{6,2},{7,3},{12,8},{13,9},{14,10},{15,11},{20,16},{21,... | collective-permute-start | bytes 1572872 | tf_op jit(solution)/shard_map/ppermute | solution.py:17
  95.5 12.4 %copy-start.4 = (f32[16,16,16,128]{3,2,1,0:T(8,128)S(1)}, f32[16,16,16,128]{3,2,1,0:T(8,128)}, u32[]{:S(2)}) copy-start(f32[16,16,16,128]{3,2,1,0:T(8,128)} %copy-done.3) | copy-start | bytes 6291460
  102.3 28.1 %collective-permute-start.10 = (bf16[16,4,8,64]{3,0,2,1:T(8,128)(2,1)}, bf16[16,4,8,64]{3,0,2,1:T(8,128)(2,1)S(1)}, u32[]{:S(2)}, u32[]{:S(2)}) collective-permute-start(bf16[16,4,8,64]{3,0,2,1:T(8,128)(2,1)} %get-tuple-element.13), channel_id=1, source_target_pairs={{0,1},{1,2},{2,3},{4,5},{5,6},{6,7},{8,9},{9,10},{10,11},{12,13},{... | collective-permute-start | bytes 196616 | tf_op jit(solution)/shard_map/ppermute | solution.py:15
  105.7 24.7 %collective-permute-start.11 = (bf16[16,4,8,64]{3,0,2,1:T(8,128)(2,1)}, bf16[16,4,8,64]{3,0,2,1:T(8,128)(2,1)S(1)}, u32[]{:S(2)}, u32[]{:S(2)}) collective-permute-start(bf16[16,4,8,64]{3,0,2,1:T(8,128)(2,1)} %get-tuple-element.14), channel_id=1, source_target_pairs={{1,0},{2,1},{3,2},{5,4},{6,5},{7,6},{9,8},{10,9},{11,10},{13,12},{... | collective-permute-start | bytes 196616 | tf_op jit(solution)/shard_map/ppermute | solution.py:17
  107.1 0.8 copy-start.7
  119.5 47.9 %collective-permute-start.4 = (f32[16,4,16,128]{3,2,1,0:T(8,128)}, f32[16,4,16,128]{3,2,1,0:T(8,128)}, u32[]{:S(2)}, u32[]{:S(2)}) collective-permute-start(f32[16,4,16,128]{3,2,1,0:T(8,128)} %get-tuple-element.5), channel_id=1, source_target_pairs={{0,1},{1,2},{2,3},{4,5},{5,6},{6,7},{8,9},{9,10},{10,11},{12,13},{... | collective-permute-start | bytes 1572872 | tf_op jit(solution)/shard_map/ppermute | solution.py:15
  124.8 42.6 %collective-permute-start.5 = (f32[16,4,16,128]{3,2,1,0:T(8,128)}, f32[16,4,16,128]{3,2,1,0:T(8,128)}, u32[]{:S(2)}, u32[]{:S(2)}) collective-permute-start(f32[16,4,16,128]{3,2,1,0:T(8,128)} %get-tuple-element.6), channel_id=1, source_target_pairs={{1,0},{2,1},{3,2},{5,4},{6,5},{7,6},{9,8},{10,9},{11,10},{13,12},{... | collective-permute-start | bytes 1572872 | tf_op jit(solution)/shard_map/ppermute | solution.py:17
  167.4 10.3 %copy-start.1 = (bf16[2,2,16,2048]{3,2,1,0:T(8,128)(2,1)S(1)}, bf16[2,2,16,2048]{3,2,1,0:T(8,128)(2,1)}, u32[]{:S(2)}) copy-start(bf16[2,2,16,2048]{3,2,1,0:T(8,128)(2,1)} %param.7) | copy-start | bytes 786436
